TPU v7x, 32 devices: a whole 2x2x4 slice. The times are simulated.
32 devices in a mesh: grp: 4 (over x, core), node: 8 (over z, y).
Axes of the slice: x: 2, y: 2, z: 4, core: 2. Of those that a mesh axis runs over, the one named last changes fastest.
Arguments:
- samples: bfloat16 [16384, 512], P(('grp', 'node')), may hold values from -6 to 6
- omega: bfloat16 [16384, 512], P(('grp', 'node')), may hold values from -6 to 6
- diag_block: bfloat16 [16384, 512], P(('grp', 'node')), may hold values from -0.25 to 0.25
- leaf_pivots: int32 [32, 128], P(('grp', 'node')), may hold values from 0 to 511, as said below
- leaf_interp: bfloat16 [16384, 128], P(('grp', 'node')), may hold values from -0.25 to 0.25
- coupling: bfloat16 [4096, 128], P(('grp', 'node')), may hold values from -0.5 to 0.5
- parent_pivots: int32 [16, 128], P('grp'), may hold values from 0 to 255, as said below
- parent_interp: bfloat16 [4096, 128], P(('grp', 'node')), may hold values from -8 to 8
- far_coupling: bfloat16 [16384, 1024], P(('grp', 'node')), may hold values from -0.1875 to 0.1875
Outputs:
- parent_rows: bfloat16 [2048, 512], P(('grp', 'node'))
- transfer: bfloat16 [16384, 128], P(('grp', 'node'))
- far_field: bfloat16 [16384, 512], P(('grp', 'node'))
Inputs may be any that keep to these rules, and one draw needn't show every extreme that they name: `leaf_pivots`: the 128 entries of a row are distinct local row numbers of the leaf. `parent_pivots`: the 128 entries of a row are distinct.
All inputs are finite; a program needn't handle non-finite values.
Results may differ from a plain program's by a relative error of at most 0.01.
Values may be sent and summed in bfloat16 or wider, within the bound.
A program may use at most 64 MiB of HBM per device.

v0:
```python
import jax
import jax.numpy as jnp
from jax import lax
from jax.sharding import PartitionSpec as P


def swapped(block, axis, stride):
    count = lax.axis_size(axis)
    route = []
    for low in range(count):
        high = low | 1 << stride
        if high != low and high < count:
            route += [(low, high), (high, low)]
    return lax.ppermute(block, axis, route)


def shards(
    samples,
    omega,
    diag_block,
    leaf_pivots,
    leaf_interp,
    coupling,
    parent_pivots,
    parent_interp,
    far_coupling,
):
    pivots_own = leaf_pivots[0]
    rank_size = pivots_own.shape[0]
    half_rows = rank_size // 2
    diag_rows = jnp.take(diag_block, pivots_own, axis=0)
    sample_rows = jnp.take(samples, pivots_own, axis=0)
    skeleton = (
        sample_rows.astype(jnp.float32)
        - jnp.dot(diag_rows, omega, preferred_element_type=jnp.float32)
    ).astype(jnp.bfloat16)
    compressed = jnp.einsum(
        "mk,ms->ks", leaf_interp, omega, preferred_element_type=jnp.float32
    ).astype(jnp.bfloat16)
    compressed_sib = swapped(compressed, "node", 0)
    reduced = (
        skeleton.astype(jnp.float32)
        - jnp.dot(coupling, compressed_sib, preferred_element_type=jnp.float32)
    ).astype(jnp.bfloat16)
    reduced_sib = swapped(reduced, "node", 0)
    position = lax.axis_index("node")
    parity = position % 2
    merged = jnp.where(
        parity == 0,
        jnp.concatenate([reduced, reduced_sib], axis=0),
        jnp.concatenate([reduced_sib, reduced], axis=0),
    )
    parent_slot = position // 2
    parent_cols = lax.dynamic_slice_in_dim(parent_pivots, parent_slot, 1, 0)[0]
    chosen = lax.dynamic_slice_in_dim(parent_cols, parity * half_rows, half_rows, 0)
    parent_half = jnp.take(merged, chosen, axis=0)
    transfer = jnp.dot(leaf_interp, parent_interp, preferred_element_type=jnp.float32).astype(
        jnp.bfloat16
    )
    own_width = far_coupling.shape[1] // 2
    gathered = lax.all_gather(parent_half, "node", axis=0, tiled=True)
    sibling_group = swapped(gathered, "grp", 0)
    far_field = jnp.dot(
        far_coupling[:, :own_width], gathered, preferred_element_type=jnp.float32
    ) + jnp.dot(far_coupling[:, own_width:], sibling_group, preferred_element_type=jnp.float32)
    return (parent_half, transfer, far_field.astype(jnp.bfloat16))


def solution(mesh):
    placed = (
        P(("grp", "node"), None),
        P(("grp", "node"), None),
        P(("grp", "node"), None),
        P(("grp", "node"), None),
        P(("grp", "node"), None),
        P(("grp", "node"), None),
        P("grp", None),
        P(("grp", "node"), None),
        P(("grp", "node"), None),
    )
    return jax.shard_map(
        shards,
        mesh=mesh,
        in_specs=placed,
        out_specs=(P(("grp", "node"), None), P(("grp", "node"), None), P(("grp", "node"), None)),
        check_vma=False,
    )
```

profile of v0, /device:TPU:0, one launch (start us, length us, event | category | flops | bytes accessed | tf_op | source)
XLA Modules:
  0.0 51.1 jit_solution(15451527293276565346)
XLA Ops:
  0.6 0.0 copy-start
  0.7 1.0 %copy-done = bf16[512,512]{1,0:T(8,128)(2,1)S(1)} copy-done((bf16[512,512]{1,0:T(8,128)(2,1)S(1)}, bf16[512,512]{1,0:T(8,128)(2,1)}, u32[]{:S(2)}) %copy-start) | copy-done | bytes 524312
  1.7 1.1 %convolution_convert_fusion = bf16[128,512]{1,0:T(8,128)(2,1)S(1)} fusion(bf16[512,128]{1,0:T(8,128)(2,1)} %param.15, bf16[512,512]{1,0:T(8,128)(2,1)S(1)} %copy-done), kind=kOutput, calls=%fused_computation.12 | convolution fusion | flops 67174400 | bytes 786432 | tf_op jit(solution)/shard_map/mk,ms->ks/dot_general | solution.py:37
  2.8 3.1 %collective-permute-start = (bf16[128,512]{1,0:T(8,128)(2,1)S(1)}, bf16[128,512]{1,0:T(8,128)(2,1)S(1)}, u32[]{:S(2)}, u32[]{:S(2)}) collective-permute-start(bf16[128,512]{1,0:T(8,128)(2,1)S(1)} %convolution_convert_fusion), channel_id=1, source_target_pairs={{0,1},{1,0},{2,3},{3,2},{4,5},{5,4},{6,7},{7,6},{8,9},{9,8},{10,11... | collective-permute-start | bytes 393224 | tf_op jit(solution)/shard_map/ppermute | solution.py:14
  5.9 0.0 copy-start.2
  5.9 0.8 %gather_fusion.1 = bf16[128,512]{1,0:T(8,128)(2,1)S(1)} fusion(bf16[512,512]{1,0:T(8,128)(2,1)S(1)} %copy-done.1, s32[1024]{0:T(1024)S(1)} %pad_clamp_fusion.1), kind=kCustom, calls=%fused_computation.clone | custom fusion | bytes 262656 | tf_op jit(solution)/shard_map/jit(_take)/gather | solution.py:32
  6.8 0.2 copy-done.2
  7.0 0.8 %gather_fusion.2 = bf16[128,512]{1,0:T(8,128)(2,1)S(1)} fusion(bf16[512,512]{1,0:T(8,128)(2,1)S(1)} %copy-done.2, s32[1024]{0:T(1024)S(1)} %pad_clamp_fusion.1), kind=kCustom, calls=%fused_computation.1.clone | custom fusion | bytes 262656 | tf_op jit(solution)/shard_map/jit(_take)/gather | solution.py:31
  7.8 0.3 fusion.5
  8.1 0.0 copy-start.6
  8.2 0.0 copy-start.8
  8.2 0.7 %copy-done.8 = s32[4,128]{1,0:T(4,128)S(1)} copy-done((s32[4,128]{1,0:T(4,128)S(1)}, s32[4,128]{1,0:T(4,128)}, u32[]{:S(2)}) %copy-start.8) | copy-done | bytes 2072
  8.8 0.1 fusion.12
  8.9 0.5 collective-permute-done
  9.4 0.2 fusion.3
  9.6 1.8 %collective-permute-start.1 = (bf16[128,512]{1,0:T(8,128)(2,1)S(1)}, bf16[128,512]{1,0:T(8,128)(2,1)S(1)}, u32[]{:S(2)}, u32[]{:S(2)}) collective-permute-start(bf16[128,512]{1,0:T(8,128)(2,1)S(1)} %fusion.3), channel_id=1, source_target_pairs={{0,1},{1,0},{2,3},{3,2},{4,5},{5,4},{6,7},{7,6},{8,9},{9,8},{10,11... | collective-permute-start | bytes 393224 | tf_op jit(solution)/shard_map/ppermute | solution.py:14
  11.4 0.1 compare_and_fusion.1
  11.5 0.0 copy-start.3
  11.5 3.1 %collective-permute-done.1 = bf16[128,512]{1,0:T(8,128)(2,1)S(1)} collective-permute-done((bf16[128,512]{1,0:T(8,128)(2,1)S(1)}, bf16[128,512]{1,0:T(8,128)(2,1)S(1)}, u32[]{:S(2)}, u32[]{:S(2)}) %collective-permute-start.1) | collective-permute-done | bytes 131104 | tf_op jit(solution)/shard_map/ppermute | solution.py:14
  14.6 0.1 maximum_select_fusion
  14.7 0.7 %gather_fusion = bf16[64,512]{1,0:T(8,128)(2,1)S(1)} fusion(bf16[256,512]{1,0:T(8,128)(2,1)S(1)} %maximum_select_fusion, s32[1024]{0:T(1024)S(1)} %pad_clamp_fusion), kind=kCustom, calls=%fused_computation.2 | custom fusion | bytes 131328 | tf_op jit(solution)/shard_map/jit(_take)/gather | solution.py:56
  15.4 0.1 broadcast_select_fusion
  15.5 0.0 copy-start.5
  15.5 0.0 copy-start.4
  15.5 0.0 copy-start.7
  15.5 32.2 %all_gather.3 = bf16[512,512]{1,0:T(8,128)(2,1)S(1)} all-gather(bf16[64,512]{1,0:T(8,128)(2,1)S(1)} %broadcast_select_fusion), channel_id=1, replica_groups=mesh['grp'=4,'node'=8] {'node'}, dimensions={0}, use_global_device_ids=true | all-gather | bytes 589824 | tf_op jit(solution)/shard_map/all_gather | solution.py:61
  47.7 0.0 collective-permute-start.2
  47.7 0.8 %convolution_convert_fusion.1 = bf16[512,128]{1,0:T(8,128)(2,1)} fusion(bf16[512,128]{1,0:T(8,128)(2,1)S(1)} %copy-done.4, bf16[128,128]{1,0:T(8,128)(2,1)S(1)} %copy-done.7), kind=kOutput, calls=%fused_computation.13 | convolution fusion | flops 16842752 | bytes 294912 | tf_op jit(solution)/shard_map/dot_general | solution.py:57
  48.6 0.5 fusion.7
  49.0 0.6 %collective-permute-done.2 = bf16[512,512]{1,0:T(8,128)(2,1)S(1)} collective-permute-done((bf16[512,512]{1,0:T(8,128)(2,1)S(1)}, bf16[512,512]{1,0:T(8,128)(2,1)S(1)}, u32[]{:S(2)}, u32[]{:S(2)}) %collective-permute-start.2) | collective-permute-done | bytes 524320 | tf_op jit(solution)/shard_map/ppermute | solution.py:14
  49.6 0.5 fusion.1
  50.1 1.0 %copy.12 = bf16[512,512]{1,0:T(8,128)(2,1)} copy(bf16[512,512]{0,1:T(8,128)(2,1)S(1)} %fusion.1) | data formatting | bytes 1048576
  (13 shorter events, 0.0 us)
Async XLA Ops:
  0.6 1.0 %copy-start = (bf16[512,512]{1,0:T(8,128)(2,1)S(1)}, bf16[512,512]{1,0:T(8,128)(2,1)}, u32[]{:S(2)}) copy-start(bf16[512,512]{1,0:T(8,128)(2,1)} %param.12) | copy-start | bytes 1572868
  0.6 5.3 %copy-start.9 = (s32[1,128]{1,0:T(1,128)S(1)}, s32[1,128]{1,0:T(1,128)}, u32[]{:S(2)}) copy-start(s32[1,128]{1,0:T(1,128)} %param.14) | copy-start | bytes 1540
  0.7 5.3 %copy-start.1 = (bf16[512,512]{1,0:T(8,128)(2,1)S(1)}, bf16[512,512]{1,0:T(8,128)(2,1)}, u32[]{:S(2)}) copy-start(bf16[512,512]{1,0:T(8,128)(2,1)} %param.11) | copy-start | bytes 1572868
  2.8 6.6 %collective-permute-start = (bf16[128,512]{1,0:T(8,128)(2,1)S(1)}, bf16[128,512]{1,0:T(8,128)(2,1)S(1)}, u32[]{:S(2)}, u32[]{:S(2)}) collective-permute-start(bf16[128,512]{1,0:T(8,128)(2,1)S(1)} %convolution_convert_fusion), channel_id=1, source_target_pairs={{0,1},{1,0},{2,3},{3,2},{4,5},{5,4},{6,7},{7,6},{8,9},{9,8},{10,11... | collective-permute-start | bytes 393224 | tf_op jit(solution)/shard_map/ppermute | solution.py:14
  5.9 1.0 %copy-start.2 = (bf16[512,512]{1,0:T(8,128)(2,1)S(1)}, bf16[512,512]{1,0:T(8,128)(2,1)}, u32[]{:S(2)}) copy-start(bf16[512,512]{1,0:T(8,128)(2,1)} %param.13) | copy-start | bytes 1572868
  8.1 1.3 %copy-start.6 = (bf16[128,128]{1,0:T(8,128)(2,1)S(1)}, bf16[128,128]{1,0:T(8,128)(2,1)}, u32[]{:S(2)}) copy-start(bf16[128,128]{1,0:T(8,128)(2,1)} %param.16) | copy-start | bytes 98308
  8.2 0.7 %copy-start.8 = (s32[4,128]{1,0:T(4,128)S(1)}, s32[4,128]{1,0:T(4,128)}, u32[]{:S(2)}) copy-start(s32[4,128]{1,0:T(4,128)} %param.17) | copy-start | bytes 6148
  9.6 5.0 %collective-permute-start.1 = (bf16[128,512]{1,0:T(8,128)(2,1)S(1)}, bf16[128,512]{1,0:T(8,128)(2,1)S(1)}, u32[]{:S(2)}, u32[]{:S(2)}) collective-permute-start(bf16[128,512]{1,0:T(8,128)(2,1)S(1)} %fusion.3), channel_id=1, source_target_pairs={{0,1},{1,0},{2,3},{3,2},{4,5},{5,4},{6,7},{7,6},{8,9},{9,8},{10,11... | collective-permute-start | bytes 393224 | tf_op jit(solution)/shard_map/ppermute | solution.py:14
  11.5 37.1 %copy-start.3 = (bf16[512,1024]{1,0:T(8,128)(2,1)S(1)}, bf16[512,1024]{1,0:T(8,128)(2,1)}, u32[]{:S(2)}) copy-start(bf16[512,1024]{1,0:T(8,128)(2,1)} %param.19) | copy-start | bytes 3145732
  15.5 32.3 %copy-start.5 = (bf16[64,512]{1,0:T(8,128)(2,1)}, bf16[64,512]{1,0:T(8,128)(2,1)S(1)}, u32[]{:S(2)}) copy-start(bf16[64,512]{1,0:T(8,128)(2,1)S(1)} %broadcast_select_fusion) | copy-start | bytes 196612
  15.5 32.2 %copy-start.4 = (bf16[512,128]{1,0:T(8,128)(2,1)S(1)}, bf16[512,128]{1,0:T(8,128)(2,1)}, u32[]{:S(2)}) copy-start(bf16[512,128]{1,0:T(8,128)(2,1)} %param.15) | copy-start | bytes 393220
  15.5 32.2 %copy-start.7 = (bf16[128,128]{1,0:T(8,128)(2,1)S(1)}, bf16[128,128]{1,0:T(8,128)(2,1)}, u32[]{:S(2)}) copy-start(bf16[128,128]{1,0:T(8,128)(2,1)} %param.18) | copy-start | bytes 98308
  47.7 1.9 %collective-permute-start.2 = (bf16[512,512]{1,0:T(8,128)(2,1)S(1)}, bf16[512,512]{1,0:T(8,128)(2,1)S(1)}, u32[]{:S(2)}, u32[]{:S(2)}) collective-permute-start(bf16[512,512]{1,0:T(8,128)(2,1)S(1)} %all_gather.3), channel_id=1, source_target_pairs={{0,8},{8,0},{16,24},{24,16},{1,9},{9,1},{17,25},{25,17},{2,10},{10... | collective-permute-start | bytes 1572872 | tf_op jit(solution)/shard_map/ppermute | solution.py:14
where the time goes:
time: 51.4 us; the launch traced here: 51.1 us
  blocking collectives  32.2 us (63%)
  local copies, waits for them, and re-layouts  5.32 us (10%)
  starting transfers between devices  4.87 us (9%)
  waiting for transfers between devices  4.19 us (8%)
  matrix products  3.39 us (7%)
  between operations  0.83 us (2%)
    all_gather x1, blocking collectives, shards(): gathered = lax.all_gather(parent_half, 'node', axis=0, tiled=True)  32.2 us
    ppermute x3, starting transfers between devices, swapped(): return lax.ppermute(block, axis, route)  4.87 us
    ppermute x3, waiting for transfers between devices, swapped(): return lax.ppermute(block, axis, route)  4.19 us
    unnamed x21, local copies, waits for them, and re-layouts  2.92 us
    dot_general x1, matrix products, shards(): jnp.einsum('mk,ms->ks', leaf_interp, omega, preferred_element_type=jnp.fl...  1.15 us
  transfers between devices with their start and end apart: 3, of which 3 were waited for; matrix products, arithmetic and copies ran while one was open for 7% of the time, Pallas kernels for 0%

commit v1 on v0

v1 whole, which is shorter than its diff:
```python
import functools

import jax
import jax.numpy as jnp
from jax import lax
from jax.experimental import pallas as pl
from jax.experimental.pallas import tpu as pltpu
from jax.sharding import PartitionSpec as P

MESH = pl.DeviceIdType.MESH
F32 = jnp.float32
BF16 = jnp.bfloat16


def tdot(a, b):
    return lax.dot_general(a, b, (((0,), (0,)), ((), ())), preferred_element_type=F32)


def dot(a, b):
    return jnp.dot(a, b, preferred_element_type=F32)


def partner(pair, d, pairs):
    if pairs & (pairs - 1):
        return lax.rem(pair + d, pairs)
    out, bit = pair, 1
    while bit < pairs:
        if d & bit:
            out = out + bit - 2 * bit * lax.rem(pair // bit, 2)
        bit *= 2
    return out


def kernel(
    pairs,
    chunks,
    samples,
    omega,
    diag,
    leaf_piv,
    interp,
    coupling,
    par_piv,
    par_interp,
    far,
    rows_out,
    transfer_out,
    far_out,
    samples_v,
    omega_v,
    diag_v,
    interp_v,
    coup_v,
    par_interp_v,
    far_v,
    u_mine,
    u_sib,
    own_q,
    sib_q,
    rows_v,
    transfer_v,
    far_o,
    load_sem,
    coup_sem,
    u_sem,
    z_send,
    z_recv,
    y_send,
    y_recv,
    c_send,
    c_recv,
    p_sem,
    out_sem,
):
    grp, node = lax.axis_index("grp"), lax.axis_index("node")
    pair, parity = node // 2, lax.rem(node, 2)
    node_sib = node + 1 - 2 * parity
    grp_sib = grp + 1 - 2 * lax.rem(grp, 2)
    rank = leaf_piv.shape[1]
    half = rank // 2
    m = omega.shape[0]
    width = omega.shape[1] // chunks
    others = [partner(pair, d, pairs) for d in range(1, pairs)]

    barrier = pltpu.get_barrier_semaphore()
    pl.semaphore_signal(barrier, inc=1, device_id=(grp, node_sib), device_id_type=MESH)
    pl.semaphore_signal(barrier, inc=1, device_id=(grp_sib, node), device_id_type=MESH)
    for other in others:
        pl.semaphore_signal(
            barrier, inc=1, device_id=(grp, 2 * other + parity), device_id_type=MESH
        )

    loads = []
    for at, (src, dst) in enumerate(
        (
            (interp, interp_v),
            (omega, omega_v),
            (diag, diag_v),
            (samples, samples_v),
            (par_interp, par_interp_v),
            (far, far_v),
        )
    ):
        loads.append(pltpu.make_async_copy(src, dst, load_sem.at[at]))
        loads[-1].start()

    pl.semaphore_wait(barrier, pairs + 1)

    def remote(src, dst, send, recv, where):
        return pltpu.make_async_remote_copy(
            src_ref=src,
            dst_ref=dst,
            send_sem=send,
            recv_sem=recv,
            device_id=where,
            device_id_type=MESH,
        )

    sent = []

    def send(src, dst, s, r, where):
        copy = remote(src, dst, s, r, where)
        copy.start()
        sent.append(copy)
        return copy

    coup_copy = send(coupling, coup_v, coup_sem.at[0], coup_sem.at[1], (grp, node_sib))

    leaf_sel = (lax.broadcasted_iota(jnp.int32, (m, rank), 0) == leaf_piv[...]).astype(F32).astype(BF16)
    slots = par_piv[pl.ds(pair, 1), :]
    rows = lax.broadcasted_iota(jnp.int32, (rank, rank), 0)
    own_sel = (rows + parity * rank == slots).astype(F32).astype(BF16)
    sib_sel = (rows + (1 - parity) * rank == slots).astype(F32).astype(BF16)
    pick = dot(leaf_sel, own_sel).astype(BF16)

    loads[0].wait()
    loads[1].wait()
    compressed = tdot(interp_v[...], omega_v[...]).astype(BF16)
    loads[2].wait()
    diag_rows = tdot(pick, diag_v[...]).astype(BF16)
    loads[3].wait()
    skeleton = tdot(pick, samples_v[...]) - dot(diag_rows, omega_v[...])
    coup_copy.wait_recv()
    coup_rows = tdot(sib_sel, coup_v[...]).astype(BF16)
    u_copies = []
    for k in range(chunks):
        cols = slice(k * width, (k + 1) * width)
        u_mine[k] = (skeleton[:, cols] - dot(coup_rows, compressed[:, cols])).astype(BF16)
        u_copies.append(
            send(u_mine.at[k], u_sib.at[k], u_sem.at[0, k], u_sem.at[1, k], (grp, node_sib))
        )

    loads[4].wait()
    transfer_v[...] = dot(interp_v[...], par_interp_v[...]).astype(BF16)
    outs = [pltpu.make_async_copy(transfer_v, transfer_out, out_sem.at[0])]
    outs[0].start()

    def place(q, k, p, h=None):
        if h is None:
            return q.at[k, pl.ds(pl.multiple_of(p * rank, rank), rank), :]
        return q.at[k, pl.ds(pl.multiple_of(p * rank + h * half, half), half), :]

    p_copies = []
    for k in range(chunks):
        cols = slice(k * width, (k + 1) * width)
        u_copies[k].wait_recv()
        merged = (u_mine[k].astype(F32) + u_sib[k].astype(F32)).astype(BF16)
        own_q[k, pl.ds(pl.multiple_of(pair * rank, rank), rank), :] = merged
        spot = place(own_q, k, pair, parity)
        for other in others:
            send(
                spot,
                spot,
                z_send.at[k, other],
                z_recv.at[k, pair],
                (grp, 2 * other + parity),
            )
        p_copies.append(
            send(
                place(own_q, k, pair),
                place(sib_q, k, pair),
                p_sem.at[0, k],
                p_sem.at[1, k],
                (grp_sib, node),
            )
        )
        rows_v[:, cols] = own_q[
            k, pl.ds(pl.multiple_of(pair * rank + parity * half, half), half), :
        ]
    outs.append(pltpu.make_async_copy(rows_v, rows_out, out_sem.at[1]))
    outs[1].start()

    for k in range(chunks):
        for other in others:
            spot = place(own_q, k, other, parity)
            remote(
                spot, spot, z_send.at[k, other], z_recv.at[k, other], (grp, node_sib)
            ).wait_recv()
            send(spot, spot, y_send.at[k, other], y_recv.at[k, other], (grp, node_sib))
            send(
                spot,
                place(sib_q, k, other, parity),
                c_send.at[k, other, 0],
                c_recv.at[k, other, 0],
                (grp_sib, node),
            )

    loads[5].wait()
    own_width = far.shape[1] // 2
    parts = []
    for k in range(chunks):
        for other in others:
            spot = place(own_q, k, other, 1 - parity)
            remote(
                spot, spot, y_send.at[k, other], y_recv.at[k, other], (grp, node_sib)
            ).wait_recv()
            send(
                spot,
                place(sib_q, k, other, 1 - parity),
                c_send.at[k, other, 1],
                c_recv.at[k, other, 1],
                (grp_sib, node),
            )
        far_o[k] = dot(far_v[:, :own_width], own_q[k])
    for k in range(chunks):
        cols = slice(k * width, (k + 1) * width)
        p_copies[k].wait_recv()
        for other in others:
            for h in range(2):
                spot = place(sib_q, k, other, parity + h - 2 * parity * h)
                remote(
                    spot,
                    spot,
                    c_send.at[k, other, h],
                    c_recv.at[k, other, h],
                    (grp_sib, node),
                ).wait_recv()
        samples_v[:, cols] = (far_o[k] + dot(far_v[:, own_width:], sib_q[k])).astype(BF16)
        copy = pltpu.make_async_copy(
            samples_v.at[:, pl.ds(k * width, width)],
            far_out.at[:, pl.ds(k * width, width)],
            out_sem.at[2 + k],
        )
        copy.start()
        outs.append(copy)
    for copy in sent:
        copy.wait_send()
    for copy in outs:
        copy.wait()


def shards(chunks, *args):
    samples, omega, diag, leaf_piv, interp, coupling, par_piv, par_interp, far = args
    pairs = lax.axis_size("node") // 2
    rank = leaf_piv.shape[1]
    m, s = omega.shape
    width = s // chunks
    group = pairs * rank
    anywhere = pl.BlockSpec(memory_space=pl.ANY)
    vmem = pl.BlockSpec(memory_space=pltpu.VMEM)
    dma = pltpu.SemaphoreType.DMA
    return pl.pallas_call(
        functools.partial(kernel, pairs, chunks),
        out_shape=(
            jax.ShapeDtypeStruct((rank // 2, s), BF16),
            jax.ShapeDtypeStruct((m, rank), BF16),
            jax.ShapeDtypeStruct((m, s), BF16),
        ),
        in_specs=[anywhere, anywhere, anywhere, vmem, anywhere, anywhere, vmem, anywhere, anywhere],
        out_specs=(anywhere, anywhere, anywhere),
        scratch_shapes=[
            pltpu.VMEM((m, s), BF16),
            pltpu.VMEM((m, s), BF16),
            pltpu.VMEM((m, m), BF16),
            pltpu.VMEM((m, rank), BF16),
            pltpu.VMEM((rank, rank), BF16),
            pltpu.VMEM((rank, rank), BF16),
            pltpu.VMEM(far.shape, BF16),
            pltpu.VMEM((chunks, rank, width), BF16),
            pltpu.VMEM((chunks, rank, width), BF16),
            pltpu.VMEM((chunks, group, width), BF16),
            pltpu.VMEM((chunks, group, width), BF16),
            pltpu.VMEM((rank // 2, s), BF16),
            pltpu.VMEM((m, rank), BF16),
            pltpu.VMEM((chunks, m, width), F32),
            dma((6,)),
            dma((2,)),
            dma((2, chunks)),
            dma((chunks, pairs)),
            dma((chunks, pairs)),
            dma((chunks, pairs)),
            dma((chunks, pairs)),
            dma((chunks, pairs, 2)),
            dma((chunks, pairs, 2)),
            dma((2, chunks)),
            dma((2 + chunks,)),
        ],
        compiler_params=pltpu.CompilerParams(
            collective_id=0, has_side_effects=True, vmem_limit_bytes=60 * 1024 * 1024
        ),
        name="merge_level",
    )(*args)


def solution(mesh):
    split = P(("grp", "node"), None)
    return jax.shard_map(
        functools.partial(shards, 2),
        mesh=mesh,
        in_specs=(split, split, split, split, split, split, P("grp", None), split, split),
        out_specs=(split, split, split),
        check_vma=False,
    )
```

time: 51.4 us -> 28.4 us (0.55)
  blocking collectives: 32.2 us -> 0 us
  Pallas kernels: 0 us -> 23.5 us
  starting transfers between devices: 4.87 us -> 0 us
  waiting for transfers between devices: 4.19 us -> 0 us
  matrix products: 3.39 us -> 0 us
  local copies, waits for them, and re-layouts: 5.32 us -> 4.04 us
    all_gather x1 -> x0, blocking collectives: 32.2 us -> none  [shards(): gathered = lax.all_gather(parent_half, 'node', axis=0, tiled=True)]
    pallas_call x0 -> x1, Pallas kernels: none -> 23.5 us  [shards(): pl.pallas_call(functools.partial(kernel, pairs, chunks), out_shape=(jax.S...]
    ppermute x3 -> x0, starting transfers between devices: 4.87 us -> none  [swapped(): return lax.ppermute(block, axis, route)]
    ppermute x3 -> x0, waiting for transfers between devices: 4.19 us -> none  [swapped(): return lax.ppermute(block, axis, route)]
    dot_general x6 -> x0, matrix products: 3.39 us -> none  [the longest x1 1.15 us: shards(): jnp.einsum('mk,ms->ks', leaf_interp, omega, preferred_element_type=jnp.fl...]
    gather x3 -> x0, local copies, waits for them, and re-layouts: 2.4 us -> none  [the longest x1 0.85 us: shards(): sample_rows = jnp.take(samples, pivots_own, axis=0)]
    unnamed x21 -> x5, local copies, waits for them, and re-layouts: 2.92 us -> 4.04 us
  transfers between devices with their start and end apart: 3 -> 0, of which waited for: 3 -> 0; matrix products, arithmetic and copies ran while one was open for 7% -> 0% of each run, Pallas kernels for 0% -> 0%
where the time goes in v1:
time: 28.4 us; the launch traced here: 28.1 us
  Pallas kernels  23.5 us (83%)
  local copies, waits for them, and re-layouts  4.04 us (14%)
  between operations  0.65 us (2%)
    pallas_call x1, Pallas kernels, shards(): pl.pallas_call(functools.partial(kernel, pairs, chunks), out_shape=(jax.S...  23.5 us
    unnamed x5, local copies, waits for them, and re-layouts  4.04 us

profile of v1, /device:TPU:0, one launch (start us, length us, event | category | flops | bytes accessed | tf_op | source)
XLA Modules:
  0.0 28.1 jit_solution(2721789669369729696)
XLA Ops:
  0.6 23.5 %merge_level.1 = (bf16[64,512]{1,0:T(8,128)(2,1)}, bf16[512,128]{1,0:T(8,128)(2,1)}, bf16[512,512]{1,0:T(8,128)(2,1)}) custom-call(bf16[512,512]{1,0:T(8,128)(2,1)} %samples.1, bf16[512,512]{1,0:T(8,128)(2,1)} %omega.1, bf16[512,512]{1,0:T(8,128)(2,1)} %diag.1, s32[1,128]{1,0:T(1,128)} %leaf_piv.1, bf16[512,128]{1,0:T(8,128)(2,1)} %interp.1, ...), custom_call_target="tpu_custom_call" | custom-call | tf_op jit(solution)/shard_map/merge_level/pallas_call | solution.py:262
  24.1 0.0 copy-start
  24.1 1.5 %copy.15 = bf16[64,512]{1,0:T(8,128)(2,1)} copy(bf16[64,512]{1,0:T(8,128)(2,1)} %get-tuple-element.6) | data formatting | bytes 131072
  25.6 0.0 copy-done
  25.6 0.7 %copy.16 = bf16[512,128]{1,0:T(8,128)(2,1)} copy(bf16[512,128]{1,0:T(8,128)(2,1)S(1)} %copy-done) | data formatting | bytes 262144
  26.3 1.9 %copy.17 = bf16[512,512]{1,0:T(8,128)(2,1)} copy(bf16[512,512]{1,0:T(8,128)(2,1)} %get-tuple-element.8) | data formatting | bytes 1048576
Async XLA Ops:
  24.1 1.5 %copy-start = (bf16[512,128]{1,0:T(8,128)(2,1)S(1)}, bf16[512,128]{1,0:T(8,128)(2,1)}, u32[]{:S(2)}) copy-start(bf16[512,128]{1,0:T(8,128)(2,1)} %get-tuple-element.7) | copy-start | bytes 393220

commit v2 on v1

--- a/solution.py
+++ b/solution.py
@@ -43,9 +43,9 @@
     par_piv,
     par_interp,
     far,
-    rows_out,
-    transfer_out,
-    far_out,
+    rows_v,
+    transfer_v,
+    far_done,
     samples_v,
     omega_v,
     diag_v,
@@ -57,8 +57,6 @@
     u_sib,
     own_q,
     sib_q,
-    rows_v,
-    transfer_v,
     far_o,
     load_sem,
     coup_sem,
@@ -70,7 +68,6 @@
     c_send,
     c_recv,
     p_sem,
-    out_sem,
 ):
     grp, node = lax.axis_index("grp"), lax.axis_index("node")
     pair, parity = node // 2, lax.rem(node, 2)
@@ -152,8 +149,6 @@
 
     loads[4].wait()
     transfer_v[...] = dot(interp_v[...], par_interp_v[...]).astype(BF16)
-    outs = [pltpu.make_async_copy(transfer_v, transfer_out, out_sem.at[0])]
-    outs[0].start()
 
     def place(q, k, p, h=None):
         if h is None:
@@ -187,8 +182,6 @@
         rows_v[:, cols] = own_q[
             k, pl.ds(pl.multiple_of(pair * rank + parity * half, half), half), :
         ]
-    outs.append(pltpu.make_async_copy(rows_v, rows_out, out_sem.at[1]))
-    outs[1].start()
 
     for k in range(chunks):
         for other in others:
@@ -235,17 +228,20 @@
                     c_recv.at[k, other, h],
                     (grp_sib, node),
                 ).wait_recv()
-        samples_v[:, cols] = (far_o[k] + dot(far_v[:, own_width:], sib_q[k])).astype(BF16)
-        copy = pltpu.make_async_copy(
-            samples_v.at[:, pl.ds(k * width, width)],
-            far_out.at[:, pl.ds(k * width, width)],
-            out_sem.at[2 + k],
-        )
-        copy.start()
-        outs.append(copy)
+        far_done[:, cols] = (far_o[k] + dot(far_v[:, own_width:], sib_q[k])).astype(BF16)
     for copy in sent:
         copy.wait_send()
-    for copy in outs:
+
+
+def emit(*refs):
+    count = len(refs) // 2
+    sem = refs[-1]
+    copies = [
+        pltpu.make_async_copy(refs[at], refs[count + at], sem.at[at]) for at in range(count)
+    ]
+    for copy in copies:
+        copy.start()
+    for copy in copies:
         copy.wait()
 
 
@@ -256,18 +252,15 @@
     m, s = omega.shape
     width = s // chunks
     group = pairs * rank
-    anywhere = pl.BlockSpec(memory_space=pl.ANY)
+    hbm = pl.BlockSpec(memory_space=pltpu.HBM)
     vmem = pl.BlockSpec(memory_space=pltpu.VMEM)
     dma = pltpu.SemaphoreType.DMA
-    return pl.pallas_call(
+    shapes = ((rank // 2, s), (m, rank), (m, s))
+    held = pl.pallas_call(
         functools.partial(kernel, pairs, chunks),
-        out_shape=(
-            jax.ShapeDtypeStruct((rank // 2, s), BF16),
-            jax.ShapeDtypeStruct((m, rank), BF16),
-            jax.ShapeDtypeStruct((m, s), BF16),
-        ),
-        in_specs=[anywhere, anywhere, anywhere, vmem, anywhere, anywhere, vmem, anywhere, anywhere],
-        out_specs=(anywhere, anywhere, anywhere),
+        out_shape=tuple(pltpu.VMEM(shape, BF16) for shape in shapes),
+        in_specs=[hbm, hbm, hbm, vmem, hbm, hbm, vmem, hbm, hbm],
+        out_specs=(vmem, vmem, vmem),
         scratch_shapes=[
             pltpu.VMEM((m, s), BF16),
             pltpu.VMEM((m, s), BF16),
@@ -280,8 +273,6 @@
             pltpu.VMEM((chunks, rank, width), BF16),
             pltpu.VMEM((chunks, group, width), BF16),
             pltpu.VMEM((chunks, group, width), BF16),
-            pltpu.VMEM((rank // 2, s), BF16),
-            pltpu.VMEM((m, rank), BF16),
             pltpu.VMEM((chunks, m, width), F32),
             dma((6,)),
             dma((2,)),
@@ -293,13 +284,20 @@
             dma((chunks, pairs, 2)),
             dma((chunks, pairs, 2)),
             dma((2, chunks)),
-            dma((2 + chunks,)),
         ],
         compiler_params=pltpu.CompilerParams(
             collective_id=0, has_side_effects=True, vmem_limit_bytes=60 * 1024 * 1024
         ),
         name="merge_level",
     )(*args)
+    return pl.pallas_call(
+        emit,
+        out_shape=tuple(jax.ShapeDtypeStruct(shape, BF16) for shape in shapes),
+        in_specs=[pl.BlockSpec(memory_space=pl.ANY)] * len(shapes),
+        out_specs=(hbm,) * len(shapes),
+        scratch_shapes=[dma((len(shapes),))],
+        name="emit",
+    )(*(pltpu.with_memory_space_constraint(block, pltpu.VMEM) for block in held))
 
 
 def solution(mesh):

time: 28.4 us -> 24.5 us (0.86)
  local copies, waits for them, and re-layouts: 4.04 us -> 0 us
    unnamed x5 -> x0, local copies, waits for them, and re-layouts: 4.04 us -> none
    pallas_call x1 -> x2, Pallas kernels: 23.5 us -> 23.7 us  [the longest x1 22.8 us: shards(): pl.pallas_call(functools.partial(kernel, pairs, chunks), out_shape=tuple(...]
where the time goes in v2:
time: 24.5 us; the launch traced here: 24.3 us
  Pallas kernels  23.7 us (97%)
  between operations  0.64 us (3%)
    pallas_call x1, Pallas kernels, shards(): pl.pallas_call(functools.partial(kernel, pairs, chunks), out_shape=tuple(...  22.8 us
    pallas_call x1, Pallas kernels, shards(): pl.pallas_call(emit, out_shape=tuple((jax.ShapeDtypeStruct(shape, BF16) f...  0.89 us

profile of v2, /device:TPU:0, one launch (start us, length us, event | category | flops | bytes accessed | tf_op | source)
XLA Modules:
  0.0 24.3 jit_solution(2975570084992218074)
XLA Ops:
  0.6 22.8 %merge_level.1 = (bf16[64,512]{1,0:T(8,128)(2,1)S(1)}, bf16[512,128]{1,0:T(8,128)(2,1)S(1)}, bf16[512,512]{1,0:T(8,128)(2,1)S(1)}) custom-call(bf16[512,512]{1,0:T(8,128)(2,1)} %samples.1, bf16[512,512]{1,0:T(8,128)(2,1)} %omega.1, bf16[512,512]{1,0:T(8,128)(2,1)} %diag.1, s32[1,128]{1,0:T(1,128)} %leaf_piv.1, bf16[512,128]{1,0:T(8,128)(2,1)} %interp.1, ...), custom_call_target="tpu_custom_call" | custom-call | tf_op jit(solution)/shard_map/merge_level/pallas_call | solution.py:259
  23.4 0.9 %emit.1 = (bf16[64,512]{1,0:T(8,128)(2,1)}, bf16[512,128]{1,0:T(8,128)(2,1)}, bf16[512,512]{1,0:T(8,128)(2,1)}) custom-call(bf16[64,512]{1,0:T(8,128)(2,1)S(1)} %get-tuple-element.6.refs_0_, bf16[512,128]{1,0:T(8,128)(2,1)S(1)} %get-tuple-element.7.refs_1_, bf16[512,512]{1,0:T(8,128)(2,1)S(1)} %get-tuple-element.8.refs_2_), custom_call_target="tpu_custom_call" | custom-call | tf_op jit(solution)/shard_map/emit/pallas_call | solution.py:293

commit v3 on v2

--- a/solution.py
+++ b/solution.py
@@ -18,17 +18,6 @@
 
 def dot(a, b):
     return jnp.dot(a, b, preferred_element_type=F32)
-
-
-def partner(pair, d, pairs):
-    if pairs & (pairs - 1):
-        return lax.rem(pair + d, pairs)
-    out, bit = pair, 1
-    while bit < pairs:
-        if d & bit:
-            out = out + bit - 2 * bit * lax.rem(pair // bit, 2)
-        bit *= 2
-    return out
 
 
 def kernel(
@@ -67,7 +56,7 @@
     y_recv,
     c_send,
     c_recv,
-    p_sem,
+    ready,
 ):
     grp, node = lax.axis_index("grp"), lax.axis_index("node")
     pair, parity = node // 2, lax.rem(node, 2)
@@ -77,15 +66,18 @@
     half = rank // 2
     m = omega.shape[0]
     width = omega.shape[1] // chunks
-    others = [partner(pair, d, pairs) for d in range(1, pairs)]
+    below, above = pair > 0, pair < pairs - 1
+    lower, upper = (grp, node - 2), (grp, node + 2)
 
     barrier = pltpu.get_barrier_semaphore()
-    pl.semaphore_signal(barrier, inc=1, device_id=(grp, node_sib), device_id_type=MESH)
-    pl.semaphore_signal(barrier, inc=1, device_id=(grp_sib, node), device_id_type=MESH)
-    for other in others:
-        pl.semaphore_signal(
-            barrier, inc=1, device_id=(grp, 2 * other + parity), device_id_type=MESH
-        )
+
+    def greet(where):
+        pl.semaphore_signal(barrier, inc=1, device_id=where, device_id_type=MESH)
+
+    greet((grp, node_sib))
+    greet((grp_sib, node))
+    pl.when(below)(lambda: greet(lower))
+    pl.when(above)(lambda: greet(upper))
 
     loads = []
     for at, (src, dst) in enumerate(
@@ -99,9 +91,11 @@
         )
     ):
         loads.append(pltpu.make_async_copy(src, dst, load_sem.at[at]))
-        loads[-1].start()
-
-    pl.semaphore_wait(barrier, pairs + 1)
+    for load in loads[:4]:
+        load.start()
+
+    greeted = 2 + (pair + pairs - 1) // pairs + (2 * pairs - 2 - pair) // pairs
+    pl.semaphore_wait(barrier, greeted)
 
     def remote(src, dst, send, recv, where):
         return pltpu.make_async_remote_copy(
@@ -115,13 +109,30 @@
 
     sent = []
 
-    def send(src, dst, s, r, where):
-        copy = remote(src, dst, s, r, where)
+    def send(*where):
+        copy = remote(*where)
         copy.start()
-        sent.append(copy)
+        sent.append(copy.wait_send)
         return copy
 
     coup_copy = send(coupling, coup_v, coup_sem.at[0], coup_sem.at[1], (grp, node_sib))
+
+    def at_distance(d, act):
+        pl.when(pair >= d)(lambda: act(pair - d, above, upper))
+        pl.when(pair + d < pairs)(lambda: act(pair + d, below, lower))
+
+    def tell(other, onward, where):
+        @pl.when(onward)
+        def _():
+            pl.semaphore_signal(
+                ready.at[other], inc=1, device_id=where, device_id_type=MESH
+            )
+
+    def heard(other, onward, where):
+        pl.semaphore_wait(ready.at[other], 1)
+        tell(other, onward, where)
+
+    at_distance(1, tell)
 
     leaf_sel = (lax.broadcasted_iota(jnp.int32, (m, rank), 0) == leaf_piv[...]).astype(F32).astype(BF16)
     slots = par_piv[pl.ds(pair, 1), :]
@@ -140,13 +151,21 @@
     coup_copy.wait_recv()
     coup_rows = tdot(sib_sel, coup_v[...]).astype(BF16)
     u_copies = []
+
+    def theirs(k):
+        return u_mine.at[k, pl.ds(pl.multiple_of((1 - parity) * half, half), half), :]
+
     for k in range(chunks):
         cols = slice(k * width, (k + 1) * width)
         u_mine[k] = (skeleton[:, cols] - dot(coup_rows, compressed[:, cols])).astype(BF16)
         u_copies.append(
-            send(u_mine.at[k], u_sib.at[k], u_sem.at[0, k], u_sem.at[1, k], (grp, node_sib))
+            send(theirs(k), u_sib.at[k], u_sem.at[0, k], u_sem.at[1, k], (grp, node_sib))
         )
 
+    loads[4].start()
+    loads[5].start()
+    for d in range(2, pairs):
+        at_distance(d, heard)
     loads[4].wait()
     transfer_v[...] = dot(interp_v[...], par_interp_v[...]).astype(BF16)
 
@@ -155,82 +174,83 @@
             return q.at[k, pl.ds(pl.multiple_of(p * rank, rank), rank), :]
         return q.at[k, pl.ds(pl.multiple_of(p * rank + h * half, half), half), :]
 
-    p_copies = []
+    def to_z(k, other):
+        spot = place(own_q, k, pair, parity)
+        z_here, z_there = z_send.at[k, other], z_recv.at[k, pair]
+        return remote(spot, spot, z_here, z_there, (grp, 2 * other + parity))
+
+    def arrive(k, other, sems, h):
+        spot = place(own_q, k, other, h)
+        at = sems.at[k, other]
+        remote(spot, spot, at, at, (grp, node_sib)).wait_recv()
+        return spot
+
+    def share(k, other, spot, h, side):
+        c_here, c_there = c_send.at[k, other, side], c_recv.at[k, other, side]
+        remote(spot, place(sib_q, k, other, h), c_here, c_there, (grp_sib, node)).start()
+
+    def onward(k, other):
+        spot = place(own_q, k, other, parity)
+        y_here, y_there = y_send.at[k, other], y_recv.at[k, other]
+        remote(spot, spot, y_here, y_there, (grp, node_sib)).start()
+        share(k, other, spot, parity, 0)
+
+    def from_z(k, other, *_):
+        arrive(k, other, z_recv, parity)
+        onward(k, other)
+
+    def from_y(k, other):
+        spot = arrive(k, other, y_recv, 1 - parity)
+        share(k, other, spot, 1 - parity, 1)
+
+    def drain(k, other, *_):
+        spot = place(own_q, k, other, parity)
+        y_here, y_there = y_send.at[k, other], y_recv.at[k, other]
+        remote(spot, spot, y_here, y_there, (grp, node_sib)).wait_send()
+        for side in range(2):
+            c_here, c_there = c_send.at[k, other, side], c_recv.at[k, other, side]
+            remote(spot, spot, c_here, c_there, (grp_sib, node)).wait_send()
+
+    def landed(k, other, *_):
+        for side in range(2):
+            spot = place(sib_q, k, other, parity)
+            at = c_recv.at[k, other, side]
+            remote(spot, spot, at, at, (grp_sib, node)).wait_recv()
+
     for k in range(chunks):
         cols = slice(k * width, (k + 1) * width)
         u_copies[k].wait_recv()
-        merged = (u_mine[k].astype(F32) + u_sib[k].astype(F32)).astype(BF16)
-        own_q[k, pl.ds(pl.multiple_of(pair * rank, rank), rank), :] = merged
-        spot = place(own_q, k, pair, parity)
-        for other in others:
-            send(
-                spot,
-                spot,
-                z_send.at[k, other],
-                z_recv.at[k, pair],
-                (grp, 2 * other + parity),
-            )
-        p_copies.append(
-            send(
-                place(own_q, k, pair),
-                place(sib_q, k, pair),
-                p_sem.at[0, k],
-                p_sem.at[1, k],
-                (grp_sib, node),
-            )
-        )
-        rows_v[:, cols] = own_q[
-            k, pl.ds(pl.multiple_of(pair * rank + parity * half, half), half), :
-        ]
-
-    for k in range(chunks):
-        for other in others:
-            spot = place(own_q, k, other, parity)
-            remote(
-                spot, spot, z_send.at[k, other], z_recv.at[k, other], (grp, node_sib)
-            ).wait_recv()
-            send(spot, spot, y_send.at[k, other], y_recv.at[k, other], (grp, node_sib))
-            send(
-                spot,
-                place(sib_q, k, other, parity),
-                c_send.at[k, other, 0],
-                c_recv.at[k, other, 0],
-                (grp_sib, node),
-            )
-
+        mine = u_mine[k, pl.ds(pl.multiple_of(parity * half, half), half), :]
+        merged = (mine.astype(F32) + u_sib[k].astype(F32)).astype(BF16)
+        own_q[k, pl.ds(pl.multiple_of(pair * rank + parity * half, half), half), :] = merged
+        rows_v[:, cols] = merged
+        for d in range(pairs - 1, 0, -1):
+            at_distance(d, lambda other, *_: to_z(k, other).start())
+        onward(k, pair)
+    for k in range(chunks):
+        for d in range(1, pairs):
+            at_distance(d, functools.partial(from_z, k))
     loads[5].wait()
     own_width = far.shape[1] // 2
-    parts = []
-    for k in range(chunks):
-        for other in others:
-            spot = place(own_q, k, other, 1 - parity)
-            remote(
-                spot, spot, y_send.at[k, other], y_recv.at[k, other], (grp, node_sib)
-            ).wait_recv()
-            send(
-                spot,
-                place(sib_q, k, other, 1 - parity),
-                c_send.at[k, other, 1],
-                c_recv.at[k, other, 1],
-                (grp_sib, node),
-            )
+    for k in range(chunks):
+        from_y(k, pair)
+        for d in range(1, pairs):
+            at_distance(d, lambda other, *_: from_y(k, other))
         far_o[k] = dot(far_v[:, :own_width], own_q[k])
+
     for k in range(chunks):
         cols = slice(k * width, (k + 1) * width)
-        p_copies[k].wait_recv()
-        for other in others:
-            for h in range(2):
-                spot = place(sib_q, k, other, parity + h - 2 * parity * h)
-                remote(
-                    spot,
-                    spot,
-                    c_send.at[k, other, h],
-                    c_recv.at[k, other, h],
-                    (grp_sib, node),
-                ).wait_recv()
+        landed(k, pair)
+        for d in range(1, pairs):
+            at_distance(d, functools.partial(landed, k))
         far_done[:, cols] = (far_o[k] + dot(far_v[:, own_width:], sib_q[k])).astype(BF16)
-    for copy in sent:
-        copy.wait_send()
+    for wait in sent:
+        wait()
+    for k in range(chunks):
+        drain(k, pair)
+        for d in range(1, pairs):
+            at_distance(d, lambda other, *_: to_z(k, other).wait_send())
+            at_distance(d, functools.partial(drain, k))
 
 
 def emit(*refs):
@@ -270,7 +290,7 @@
             pltpu.VMEM((rank, rank), BF16),
             pltpu.VMEM(far.shape, BF16),
             pltpu.VMEM((chunks, rank, width), BF16),
-            pltpu.VMEM((chunks, rank, width), BF16),
+            pltpu.VMEM((chunks, rank // 2, width), BF16),
             pltpu.VMEM((chunks, group, width), BF16),
             pltpu.VMEM((chunks, group, width), BF16),
             pltpu.VMEM((chunks, m, width), F32),
@@ -283,7 +303,7 @@
             dma((chunks, pairs)),
             dma((chunks, pairs, 2)),
             dma((chunks, pairs, 2)),
-            dma((2, chunks)),
+            pltpu.SemaphoreType.REGULAR((pairs,)),
         ],
         compiler_params=pltpu.CompilerParams(
             collective_id=0, has_side_effects=True, vmem_limit_bytes=60 * 1024 * 1024

time: 24.5 us -> 24.1 us (0.984)
  Pallas kernels: 23.7 us -> 23.2 us
    pallas_call x1, Pallas kernels: 22.8 us -> 22.4 us  [shards(): pl.pallas_call(functools.partial(kernel, pairs, chunks), out_shape=tuple(...]
where the time goes in v3:
time: 24.1 us; the launch traced here: 23.9 us
  Pallas kernels  23.2 us (96%)
  between operations  0.64 us (3%)
    pallas_call x1, Pallas kernels, shards(): pl.pallas_call(functools.partial(kernel, pairs, chunks), out_shape=tuple(...  22.4 us
    pallas_call x1, Pallas kernels, shards(): pl.pallas_call(emit, out_shape=tuple((jax.ShapeDtypeStruct(shape, BF16) f...  0.89 us

profile of v3, /device:TPU:0, one launch (start us, length us, event | category | flops | bytes accessed | tf_op | source)
XLA Modules:
  0.0 23.9 jit_solution(12733010095521838406)
XLA Ops:
  0.6 22.4 %merge_level.1 = (bf16[64,512]{1,0:T(8,128)(2,1)S(1)}, bf16[512,128]{1,0:T(8,128)(2,1)S(1)}, bf16[512,512]{1,0:T(8,128)(2,1)S(1)}) custom-call(bf16[512,512]{1,0:T(8,128)(2,1)} %samples.1, bf16[512,512]{1,0:T(8,128)(2,1)} %omega.1, bf16[512,512]{1,0:T(8,128)(2,1)} %diag.1, s32[1,128]{1,0:T(1,128)} %leaf_piv.1, bf16[512,128]{1,0:T(8,128)(2,1)} %interp.1, ...), custom_call_target="tpu_custom_call" | custom-call | tf_op jit(solution)/shard_map/merge_level/pallas_call | solution.py:279
  23.0 0.9 %emit.1 = (bf16[64,512]{1,0:T(8,128)(2,1)}, bf16[512,128]{1,0:T(8,128)(2,1)}, bf16[512,512]{1,0:T(8,128)(2,1)}) custom-call(bf16[64,512]{1,0:T(8,128)(2,1)S(1)} %get-tuple-element.6.refs_0_, bf16[512,128]{1,0:T(8,128)(2,1)S(1)} %get-tuple-element.7.refs_1_, bf16[512,512]{1,0:T(8,128)(2,1)S(1)} %get-tuple-element.8.refs_2_), custom_call_target="tpu_custom_call" | custom-call | tf_op jit(solution)/shard_map/emit/pallas_call | solution.py:313

commit v4 on v3

--- a/solution.py
+++ b/solution.py
@@ -42,6 +42,8 @@
     coup_v,
     par_interp_v,
     far_v,
+    leaf_piv_v,
+    par_piv_v,
     u_mine,
     u_sib,
     own_q,
@@ -88,10 +90,12 @@
             (samples, samples_v),
             (par_interp, par_interp_v),
             (far, far_v),
+            (leaf_piv, leaf_piv_v),
+            (par_piv, par_piv_v),
         )
     ):
         loads.append(pltpu.make_async_copy(src, dst, load_sem.at[at]))
-    for load in loads[:4]:
+    for load in loads[6:] + loads[:4]:
         load.start()
 
     greeted = 2 + (pair + pairs - 1) // pairs + (2 * pairs - 2 - pair) // pairs
@@ -134,8 +138,10 @@
 
     at_distance(1, tell)
 
-    leaf_sel = (lax.broadcasted_iota(jnp.int32, (m, rank), 0) == leaf_piv[...]).astype(F32).astype(BF16)
-    slots = par_piv[pl.ds(pair, 1), :]
+    loads[6].wait()
+    loads[7].wait()
+    leaf_sel = (lax.broadcasted_iota(jnp.int32, (m, rank), 0) == leaf_piv_v[...]).astype(F32).astype(BF16)
+    slots = par_piv_v[pl.ds(pair, 1), :]
     rows = lax.broadcasted_iota(jnp.int32, (rank, rank), 0)
     own_sel = (rows + parity * rank == slots).astype(F32).astype(BF16)
     sib_sel = (rows + (1 - parity) * rank == slots).astype(F32).astype(BF16)
@@ -279,7 +285,7 @@
     held = pl.pallas_call(
         functools.partial(kernel, pairs, chunks),
         out_shape=tuple(pltpu.VMEM(shape, BF16) for shape in shapes),
-        in_specs=[hbm, hbm, hbm, vmem, hbm, hbm, vmem, hbm, hbm],
+        in_specs=[hbm] * len(args),
         out_specs=(vmem, vmem, vmem),
         scratch_shapes=[
             pltpu.VMEM((m, s), BF16),
@@ -289,12 +295,14 @@
             pltpu.VMEM((rank, rank), BF16),
             pltpu.VMEM((rank, rank), BF16),
             pltpu.VMEM(far.shape, BF16),
+            pltpu.VMEM(leaf_piv.shape, leaf_piv.dtype),
+            pltpu.VMEM(par_piv.shape, par_piv.dtype),
             pltpu.VMEM((chunks, rank, width), BF16),
             pltpu.VMEM((chunks, rank // 2, width), BF16),
             pltpu.VMEM((chunks, group, width), BF16),
             pltpu.VMEM((chunks, group, width), BF16),
             pltpu.VMEM((chunks, m, width), F32),
-            dma((6,)),
+            dma((8,)),
             dma((2,)),
             dma((2, chunks)),
             dma((chunks, pairs)),

time: 24.1 us -> 23.7 us (0.983)
  Pallas kernels: 23.2 us -> 22.9 us
    pallas_call x1, Pallas kernels: 22.4 us -> 22.1 us  [shards(): pl.pallas_call(functools.partial(kernel, pairs, chunks), out_shape=tuple(...]
where the time goes in v4:
time: 23.7 us; the launch traced here: 23.6 us
  Pallas kernels  22.9 us (97%)
  between operations  0.64 us (3%)
    pallas_call x1, Pallas kernels, shards(): pl.pallas_call(functools.partial(kernel, pairs, chunks), out_shape=tuple(...  22.1 us
    pallas_call x1, Pallas kernels, shards(): pl.pallas_call(emit, out_shape=tuple((jax.ShapeDtypeStruct(shape, BF16) f...  0.89 us

profile of v4, /device:TPU:0, one launch (start us, length us, event | category | flops | bytes accessed | tf_op | source)
XLA Modules:
  0.0 23.6 jit_solution(9060696075118785676)
XLA Ops:
  0.6 22.1 %merge_level.1 = (bf16[64,512]{1,0:T(8,128)(2,1)S(1)}, bf16[512,128]{1,0:T(8,128)(2,1)S(1)}, bf16[512,512]{1,0:T(8,128)(2,1)S(1)}) custom-call(bf16[512,512]{1,0:T(8,128)(2,1)} %samples.1, bf16[512,512]{1,0:T(8,128)(2,1)} %omega.1, bf16[512,512]{1,0:T(8,128)(2,1)} %diag.1, s32[1,128]{1,0:T(1,128)} %leaf_piv.1, bf16[512,128]{1,0:T(8,128)(2,1)} %interp.1, ...), custom_call_target="tpu_custom_call" | custom-call | tf_op jit(solution)/shard_map/merge_level/pallas_call | solution.py:285
  22.7 0.9 %emit.1 = (bf16[64,512]{1,0:T(8,128)(2,1)}, bf16[512,128]{1,0:T(8,128)(2,1)}, bf16[512,512]{1,0:T(8,128)(2,1)}) custom-call(bf16[64,512]{1,0:T(8,128)(2,1)S(1)} %get-tuple-element.6.refs_0_, bf16[512,128]{1,0:T(8,128)(2,1)S(1)} %get-tuple-element.7.refs_1_, bf16[512,512]{1,0:T(8,128)(2,1)S(1)} %get-tuple-element.8.refs_2_), custom_call_target="tpu_custom_call" | custom-call | tf_op jit(solution)/shard_map/emit/pallas_call | solution.py:321
